TPU v7x, 256 devices: a whole 4x4x8 slice. The times are simulated.
256 devices in a mesh: frames: 8 (over y, x_lo), height: 32 (over x_hi, z, core).
Axes of the slice: x: 4 (x_hi: 2, x_lo: 2; x = x_hi * 2 + x_lo), y: 4, z: 8, core: 2. Of those that a mesh axis runs over, the one named last changes fastest.
Arguments:
- latent: bfloat16 [8, 64, 160, 384], P('frames', 'height'), may hold values from -15 to 15
- first_gain: float32 [384], replicated, may hold values from 0.1 to 1.9
- first_shift: float32 [384], replicated, may hold values from -4 to 4
- query_weight: bfloat16 [384, 384], replicated
- key_weight: bfloat16 [384, 384], replicated
- value_weight: bfloat16 [384, 384], replicated, may hold values from -0.3125 to 0.3125
- out_weight: bfloat16 [384, 384], replicated, may hold values from -0.3125 to 0.3125
- out_bias: float32 [384], replicated, may hold values from -6 to 6
- second_gain: float32 [384], replicated, may hold values from 0.1 to 1.9
- second_shift: float32 [384], replicated, may hold values from -4 to 4
- up_weight: bfloat16 [3, 3, 3, 384, 384], replicated, may hold values from -0.15625 to 0.15625
- up_bias: float32 [384], replicated, may hold values from -6 to 6
Outputs:
- upsampled: bfloat16 [16, 128, 320, 384], P('frames', 'height')
All inputs are finite; a program needn't handle non-finite values.
Results may differ from a plain program's by a relative error of at most 0.013.
Values may be sent and summed in bfloat16 or wider, within the bound.
A program may use at most 128 MiB of HBM per device.

v0:
```python
import jax
import jax.numpy as jnp
from jax import lax
from jax.sharding import PartitionSpec as P

GROUPS = 32


EPS = 1e-05


def passed_along(value, axis, steps):
    count = lax.axis_size(axis)
    initial, last = (max(0, -steps), min(count, count - steps))
    return lax.ppermute(value, axis, [(source, source + steps) for source in range(initial, last)])


def group_norm(value, gain, shift):
    floats = value.astype(jnp.float32)
    width = floats.shape[-1]
    per_group = width // GROUPS
    count = (
        floats.shape[0]
        * floats.shape[1]
        * floats.shape[2]
        * per_group
        * lax.axis_size("frames")
        * lax.axis_size("height")
    )

    def grouped(array):
        return jnp.sum(array, axis=(0, 1, 2)).reshape(GROUPS, per_group).sum(axis=-1)

    mean = lax.psum(grouped(floats), ("frames", "height")) / count
    centered = floats - jnp.repeat(mean, per_group)
    spread = lax.psum(grouped(centered * centered), ("frames", "height")) / count
    factor = gain * jnp.repeat(lax.rsqrt(spread + EPS), per_group)
    return centered * factor + shift


def upsample_taps(current, earlier, weight, bias):
    rows = current.shape[0] - 1
    cols = current.shape[1] - 1
    width = current.shape[2]
    time_taps = (((0, current), (2, earlier)), ((1, current),))
    space_taps = (((1, 0),), ((2, 0), (0, 1)))
    frame_list = []
    for odd_time in range(2):
        row_list = []
        for odd_row in range(2):
            col_list = []
            for odd_col in range(2):
                summed = jnp.zeros((rows * cols, width), jnp.float32)
                for time_tap, source in time_taps[odd_time]:
                    for row_tap, row_step in space_taps[odd_row]:
                        for col_tap, col_step in space_taps[odd_col]:
                            window = source[
                                row_step : row_step + rows, col_step : col_step + cols
                            ].reshape(-1, width)
                            summed = summed + jnp.dot(
                                window,
                                weight[time_tap, row_tap, col_tap],
                                preferred_element_type=jnp.float32,
                            )
                col_list.append((summed + bias).reshape(rows, cols, width))
            row_list.append(jnp.stack(col_list, axis=2).reshape(rows, 2 * cols, width))
        frame_list.append(jnp.stack(row_list, axis=1).reshape(2 * rows, 2 * cols, width))
    return jnp.stack(frame_list, axis=0)


def local(
    latent,
    first_gain,
    first_shift,
    query_weight,
    key_weight,
    value_weight,
    out_weight,
    out_bias,
    second_gain,
    second_shift,
    up_weight,
    up_bias,
):
    frames, rows, cols, width = latent.shape
    normed = group_norm(latent, first_gain, first_shift).astype(jnp.bfloat16)
    factor = width ** (-0.5)

    def project(block, weight):
        return jnp.dot(block.reshape(-1, width), weight, preferred_element_type=jnp.float32).astype(
            jnp.bfloat16
        )

    queries = project(normed, query_weight).reshape(frames, rows * cols, width)
    keys = project(normed, key_weight).reshape(frames, rows, cols, width)
    values = project(normed, value_weight).reshape(frames, rows, cols, width)
    absorb_keys = lax.all_gather(keys, "height", axis=1, tiled=True).reshape(frames, -1, width)
    absorb_values = lax.all_gather(values, "height", axis=1, tiled=True).reshape(frames, -1, width)
    highest = jnp.full((frames, rows * cols), -1e30, jnp.float32)
    scores = (
        jnp.einsum("fqc,fkc->fqk", queries, absorb_keys, preferred_element_type=jnp.float32)
        * factor
    )
    new_high = jnp.maximum(highest, jnp.max(scores, axis=-1))
    weights = jnp.exp(scores - new_high[..., None])
    totals = jnp.sum(weights, axis=-1)
    summed = jnp.einsum(
        "fqk,fkc->fqc",
        weights.astype(jnp.bfloat16),
        absorb_values,
        preferred_element_type=jnp.float32,
    )
    state = (new_high, totals, summed)
    highest, totals, summed = state
    attended = (summed / totals[..., None]).astype(jnp.bfloat16)
    branch = (
        jnp.dot(
            attended.reshape(-1, width), out_weight, preferred_element_type=jnp.float32
        ).reshape(latent.shape)
        + out_bias
    )
    mixed = (latent.astype(jnp.float32) + branch).astype(jnp.bfloat16)
    activated = jax.nn.silu(group_norm(mixed, second_gain, second_shift)).astype(jnp.bfloat16)
    cached = passed_along(activated, "frames", 1)
    earlier = jnp.concatenate([cached, activated[: frames - 1]], axis=0)
    paired = jnp.stack([activated, earlier], axis=0)
    below = passed_along(paired[:, :, :1], "height", -1)
    extended = jnp.concatenate([paired, below], axis=2)
    extended = jnp.pad(extended, ((0, 0), (0, 0), (0, 0), (0, 1), (0, 0)))
    outputs = [
        upsample_taps(extended[0, 0], extended[1, 0], up_weight, up_bias).astype(jnp.bfloat16)
    ]
    return jnp.stack(outputs, axis=0).reshape(2 * frames, 2 * rows, 2 * cols, width)


def solution(mesh):
    placed = (
        P("frames", "height", None, None),
        P(),
        P(),
        P(),
        P(),
        P(),
        P(),
        P(),
        P(),
        P(),
        P(),
        P(),
    )
    return jax.shard_map(
        local,
        mesh=mesh,
        in_specs=placed,
        out_specs=P("frames", "height", None, None),
        check_vma=False,
    )
```

profile of v0, /device:TPU:1, one launch (start us, length us, event | category | flops | bytes accessed | tf_op | source)
XLA Modules:
  0.0 571.4 jit_solution(11107464773121827469)
XLA Ops:
  7.8 81.4 %psum.28 = f32[32]{0:T(128)S(1)} all-reduce(f32[32]{0:T(128)S(1)} %reduce_sum.82), channel_id=1, replica_groups=mesh['frames'=8,'height'=32] {'frames','height'}, use_global_device_ids=true, to_apply=%region_2.0 | all-reduce | flops 32 | bytes 256 | tf_op jit(solution)/shard_map/psum | solution.py:34
  90.7 72.4 %psum.29 = f32[32]{0:T(128)S(1)} all-reduce(f32[32]{0:T(128)S(1)} %reduce_sum.84), channel_id=1, replica_groups=mesh['frames'=8,'height'=32] {'frames','height'}, use_global_device_ids=true, to_apply=%region_5.0 | all-reduce | flops 32 | bytes 256 | tf_op jit(solution)/shard_map/psum | solution.py:36
  165.0 2.0 convolution_convert_fusion.1
  167.0 2.0 convolution_convert_fusion
  169.1 93.9 %all-gather.3.cloned.1.call-done = bf16[1,64,160,384]{3,2,0,1:T(8,128)(2,1)} async-done(((bf16[1,2,160,384]{3,2,0,1:T(8,128)(2,1)}), bf16[1,64,160,384]{3,2,0,1:T(8,128)(2,1)}) %all-gather.3.cloned.1.call-update) | async-done | bytes 7864336 | tf_op jit(solution)/shard_map/all_gather | solution.py:97
  263.0 9.3 %fusion.104 = (f32[320]{0:T(512)S(1)}, f32[320,10240]{1,0:T(8,128)}) fusion(bf16[10240,384]{1,0:T(8,128)(2,1)} %bitcast.177, bf16[320,384]{1,0:T(8,128)(2,1)S(1)} %bitcast.194, bf16[384,384]{1,0:T(8,128)(2,1)S(1)} %copy-done), kind=kOutput, calls=%fused_computation.145 | convolution fusion | flops 2617630464 | bytes 21513472 | tf_op jit(solution)/shard_map/fqc,fkc->fqk/dot_general | solution.py:101
  272.2 6.9 %fusion = f32[320]{0:T(512)S(1)} fusion(f32[320,10240]{1,0:T(8,128)} %get-tuple-element.16, f32[320]{0:T(512)S(1)} %broadcast_maximum_fusion), kind=kLoop, calls=%fused_computation.2 | loop fusion | flops 6553280 | bytes 13109760 | tf_op jit(solution)/shard_map/reduce_sum | solution.py:106
  279.1 83.0 %all-gather.5.cloned.1.call-done = bf16[1,64,160,384]{3,2,0,1:T(8,128)(2,1)} async-done(((bf16[1,2,160,384]{3,2,0,1:T(8,128)(2,1)}), bf16[1,64,160,384]{3,2,0,1:T(8,128)(2,1)}) %all-gather.5.cloned.1.call-update) | async-done | bytes 7864336 | tf_op jit(solution)/shard_map/all_gather | solution.py:98
  362.1 10.6 %fusion.30 = bf16[320,384]{1,0:T(8,128)(2,1)S(1)} fusion(bf16[10240,384]{1,0:T(8,128)(2,1)} %bitcast.221, f32[320,10240]{1,0:T(8,128)} %get-tuple-element.16, f32[320]{0:T(512)S(1)} %broadcast_maximum_fusion, f32[320]{0:T(512)S(1)} %fusion), kind=kOutput, calls=%fused_computation.55 | convolution fusion | flops 2523381760 | bytes 21219840 | tf_op jit(solution)/shard_map/fqk,fkc->fqc/dot_general | solution.py:107
  373.4 74.8 %psum.30 = f32[32]{0:T(128)S(1)} all-reduce(f32[32]{0:T(128)S(1)} %reduce_sum.87), channel_id=1, replica_groups=mesh['frames'=8,'height'=32] {'frames','height'}, use_global_device_ids=true, to_apply=%region_10.0 | all-reduce | flops 32 | bytes 256 | tf_op jit(solution)/shard_map/psum | solution.py:34
  448.7 73.3 %psum.31 = f32[32]{0:T(128)S(1)} all-reduce(f32[32]{0:T(128)S(1)} %reduce_sum.89), channel_id=1, replica_groups=mesh['frames'=8,'height'=32] {'frames','height'}, use_global_device_ids=true, to_apply=%region_13.0 | all-reduce | flops 32 | bytes 256 | tf_op jit(solution)/shard_map/psum | solution.py:36
  522.4 3.0 collective-permute-start
  525.5 4.4 collective-permute-done
  530.0 3.6 collective-permute-start.1
  533.7 5.2 collective-permute-done.1
  539.3 1.5 fusion.72
  540.8 1.3 fusion.69
  542.1 1.3 fusion.64
  543.4 1.3 fusion.59
  544.7 1.3 fusion.49
  547.3 1.3 fusion.43
  555.9 1.4 pad_maximum_fusion.1
  561.5 1.4 pad_maximum_fusion.2
  563.0 1.5 pad_maximum_fusion
  (92 shorter events, 19.5 us)
Async XLA Ops:
  6.5 256.4 %copy-start = (bf16[384,384]{1,0:T(8,128)(2,1)S(1)}, bf16[384,384]{1,0:T(8,128)(2,1)}, u32[]{:S(2)}) copy-start(bf16[384,384]{1,0:T(8,128)(2,1)} %param.15) | copy-start | bytes 884740
  6.5 256.4 %all-gather.3.cloned.1.call-start = ((), (), s32[]{:S(2)}) async-start(), calls=%async_computation | async-start | bytes 8110080 | tf_op jit(solution)/shard_map/all_gather | solution.py:97
  167.0 195.1 %all-gather.5.cloned.1.call-start = ((), (), s32[]{:S(2)}) async-start(), calls=%async_computation.1 | async-start | bytes 8110080 | tf_op jit(solution)/shard_map/all_gather | solution.py:98
  362.1 10.7 %copy-start.1 = (bf16[1,2,160,384]{3,2,1,0:T(8,128)(2,1)S(1)}, bf16[1,2,160,384]{3,2,1,0:T(8,128)(2,1)}, u32[]{:S(2)}) copy-start(bf16[1,2,160,384]{3,2,1,0:T(8,128)(2,1)} %param.12) | copy-start | bytes 737284
  362.1 10.7 %copy-start.2 = (bf16[384,384]{1,0:T(8,128)(2,1)S(1)}, bf16[384,384]{1,0:T(8,128)(2,1)}, u32[]{:S(2)}) copy-start(bf16[384,384]{1,0:T(8,128)(2,1)} %param.18) | copy-start | bytes 884740
  362.1 10.7 %copy-start.5 = (f32[384]{0:T(512)S(1)}, f32[384]{0:T(512)}, u32[]{:S(2)}) copy-start(f32[384]{0:T(512)} %param.19) | copy-start | bytes 4612
  362.1 160.1 %copy-start.6 = (f32[384]{0:T(512)S(1)}, f32[384]{0:T(512)}, u32[]{:S(2)}) copy-start(f32[384]{0:T(512)} %param.20) | copy-start | bytes 4612
  362.1 160.1 %copy-start.4 = (f32[384]{0:T(512)S(1)}, f32[384]{0:T(512)}, u32[]{:S(2)}) copy-start(f32[384]{0:T(512)} %param.21) | copy-start | bytes 4612
  522.4 26.2 %slice-start = ((s8[7962624]{0:T(1024)(128)(4,1)}), s8[4194304]{0:T(1024)(128)(4,1)S(1)}, s32[]{:S(2)}) async-start(s8[7962624]{0:T(1024)(128)(4,1)} %bitcast.178), calls=%async_computation.2 | async-start | bytes 8388608
  522.4 26.2 %copy-start.3 = (f32[384]{0:T(512)S(1)}, f32[384]{0:T(512)}, u32[]{:S(2)}) copy-start(f32[384]{0:T(512)} %param.23) | copy-start | bytes 4612
  522.4 7.6 %collective-permute-start = (bf16[1,2,160,384]{3,2,1,0:T(8,128)(2,1)S(1)}, bf16[1,2,160,384]{3,2,1,0:T(8,128)(2,1)S(1)}, u32[]{:S(2)}, u32[]{:S(2)}) collective-permute-start(bf16[1,2,160,384]{3,2,1,0:T(8,128)(2,1)S(1)} %multiply_convert_fusion), channel_id=1, source_target_pairs={{0,32},{32,64},{64,96},{96,128},{128,160},{160,192},{192,224},{1,3... | collective-permute-start | bytes 737288 | tf_op jit(solution)/shard_map/ppermute | solution.py:15
  530.0 8.8 %collective-permute-start.1 = (bf16[2,1,1,160,384]{4,3,2,1,0:T(8,128)(2,1)S(1)}, bf16[2,1,1,160,384]{4,3,2,1,0:T(8,128)(2,1)S(1)}, u32[]{:S(2)}, u32[]{:S(2)}) collective-permute-start(bf16[2,1,1,160,384]{4,3,2,1,0:T(8,128)(2,1)S(1)} %pad_maximum_fusion.7), channel_id=1, source_target_pairs={{1,0},{2,1},{3,2},{4,3},{5,4},{6,5},{7,6},{8,7},{9,8},{10,9},{11,1... | collective-permute-start | bytes 737288 | tf_op jit(solution)/shard_map/ppermute | solution.py:15
  539.0 9.6 %slice-start.1 = ((s8[7962624]{0:T(1024)(128)(4,1)}), s8[3768320]{0:T(1024)(128)(4,1)S(1)}, s32[]{:S(2)}) async-start(s8[7962624]{0:T(1024)(128)(4,1)} %bitcast.178), calls=%async_computation.3 | async-start | bytes 7536640
Sparse Core Ops, SparseCore 0:
  167.1 95.7 all-gather.2
  265.7 96.3 all-gather.4
where the time goes:
time: 573 us; the launch traced here: 571 us
  blocking collectives  302 us (53%)
  waiting for transfers between devices  187 us (33%)
  matrix products  40.2 us (7%)
  other arithmetic  18.8 us (3%)
  between operations  13.9 us (2%)
  starting transfers between devices  6.66 us (1%)
    psum x2, blocking collectives, group_norm(): mean = lax.psum(grouped(floats), ('frames', 'height')) / count  156 us
    psum x2, blocking collectives, group_norm(): lax.psum(grouped(centered * centered), ('frames', 'height')) / count  146 us
    all_gather x1, waiting for transfers between devices, local(): lax.all_gather(keys, 'height', axis=1, tiled=True)  93.9 us
    all_gather x1, waiting for transfers between devices, local(): lax.all_gather(values, 'height', axis=1, tiled=True)  83 us
    dot_general x27, matrix products, upsample_taps(): jnp.dot(window, weight[time_tap, row_tap, col_tap], preferred_element_typ...  16 us
  transfers between devices with their start and end apart: 4, of which 4 were waited for; matrix products, arithmetic and copies ran while one was open for 3% of the time, Pallas kernels for 0%

commit v1 on v0

v1 whole, which is shorter than its diff:
```python
import jax
import jax.numpy as jnp
from jax import lax
from jax.experimental import pallas as pl
from jax.experimental.pallas import tpu as pltpu
from jax.sharding import PartitionSpec as P

GROUPS = 32
EPS = 1e-05
LOG2E = 1.4426950408889634
MESH = pl.DeviceIdType.MESH
BF16 = jnp.bfloat16
F32 = jnp.float32

NSLOT = 8


def make_kernel(nf, nh, rows, cols, width):
    slab = rows * cols
    half = slab // 2
    group = 16
    nx = nh // group
    total = float(nf * nh * slab)
    per_group = width // GROUPS
    lanes = width // 128

    def kernel(
        lat, g1, s1, wq, wk, wv, wo, ob, g2, s2, wup, ub, out,
        kv, xq, q2, acc, part, partin, lse, lsein, w4, wupv, vec,
        st, curm, earm, act, stage, outv,
        ssem, rsem, rs_s, rs_r, ls_s, ls_r, sib_s, sib_r, misc_s, misc_r, loc, locw, outs,
    ):
        f = lax.axis_index("frames")
        h = lax.axis_index("height")
        xh = h // group
        k = h % group
        e = f * nx + xh

        def near(j):
            return (f, xh * group + (k + j) % group)

        def far(j):
            other = (e + j) % group
            return (other // nx, (other % nx) * group + k)

        right = near(2)
        left = near(group - 2)
        sibling = (f, xh * group + k + 1 - 2 * (k % 2))
        partner = (f, (h + group) % nh)
        above = (h + nh - 1) % nh
        below = (h + 1) % nh
        later = (f + 1) % nf
        sooner = (f + nf - 1) % nf

        barrier = pltpu.get_barrier_semaphore()

        def greet(dev):
            pl.semaphore_signal(barrier, inc=1, device_id=dev, device_id_type=MESH)

        own_copy = pltpu.make_async_copy(lat, kv.at[0, pl.ds(0, slab)], loc.at[0])
        own_copy.start()

        def greet_both(j, carry):
            greet(near(j))
            greet(far(j))
            return carry

        lax.fori_loop(1, group, greet_both, 0)
        for dev in ((f, above), (f, below), (later, above), (sooner, below)):
            greet(dev)

        small = [
            pltpu.make_async_copy(src, w4.at[i], loc.at[1 + i])
            for i, src in enumerate((wq, wk, wv, wo))
        ]
        small += [
            pltpu.make_async_copy(src, vec.at[i], loc.at[5 + i])
            for i, src in enumerate((g1, s1, ob, g2, s2, ub))
        ]
        for copy in small:
            copy.start()
        up_copy = pltpu.make_async_copy(wup, wupv, locw)

        def send(src, dst, ss, rs, dev):
            return pltpu.make_async_remote_copy(
                src_ref=src, dst_ref=dst, send_sem=ss, recv_sem=rs, device_id=dev, device_id_type=MESH
            )

        def ring(step, to_right):
            hop = step // 2
            source = 0 if hop == 0 else (2 * hop - 1 if to_right else 2 * hop)
            target = 7 if hop == 3 else (2 * hop + 1 if to_right else 2 * hop + 2)
            piece = step % 2 if hop < 3 else (0 if to_right else 1)
            at = pl.ds(piece * half, half)
            ss, rs = (rs_s, rs_r) if to_right else (ls_s, ls_r)
            return send(
                kv.at[source, at], kv.at[target, at], ss.at[step], rs.at[step], right if to_right else left
            )

        rings = {(s, d): ring(s, d) for s in range(7) for d in (True, False)}
        sibs = [
            send(kv.at[s, pl.ds(0, slab)], kv.at[s, pl.ds(slab, slab)], sib_s.at[s], sib_r.at[s], sibling)
            for s in range(NSLOT)
        ]
        to_partner = send(kv.at[0, pl.ds(0, slab)], xq, misc_s.at[0], misc_r.at[0], partner)

        own_copy.wait()
        pl.semaphore_wait(barrier, 2 * (group - 1) + 4)
        for s in (0, 1):
            rings[s, True].start()
            rings[s, False].start()
        to_partner.start()
        sibs[0].start()
        up_copy.start()

        def local_stats(x, slot):
            mean = jnp.sum(x, axis=0, keepdims=True) * (1.0 / slab)
            d = x - mean
            st[slot, 0] = jnp.concatenate([mean, jnp.sum(d * d, axis=0, keepdims=True)], axis=1)

        def exchange(slot, peer, count):
            def copy(j):
                return send(
                    st.at[slot, 0], st.at[slot, j], ssem.at[slot, j], rsem.at[slot, j], peer(j)
                )

            def begin(j, carry):
                copy(j).start()
                return carry

            def finish(j, carry):
                copy(j).wait()
                return carry

            lax.fori_loop(1, group, begin, 0)
            lax.fori_loop(1, group, finish, 0)
            means = [st[slot, j, :, 0:width] for j in range(group)]
            mean = sum(means) * (1.0 / group)
            m2 = sum(st[slot, j, :, width : 2 * width] for j in range(group))
            dev = sum((one - mean) * (one - mean) for one in means)
            return mean, m2 + count * dev

        grp_row = (lax.broadcasted_iota(jnp.int32, (width, width), 0) * 5462) >> 16
        grp_col = (lax.broadcasted_iota(jnp.int32, (width, width), 1) * 5462) >> 16
        same = jnp.where(grp_row == grp_col, 1.0, 0.0).astype(F32)

        def over_group(row):
            wide = jnp.broadcast_to(row, (8, width))
            return jnp.dot(
                wide, same, precision=lax.Precision.HIGHEST, preferred_element_type=F32
            )[0:1]

        def all_stats(slot):
            mean, m2 = exchange(slot, near, float(slab))
            st[slot + 1, 0] = jnp.concatenate([mean, m2], axis=1)
            mean, m2 = exchange(slot + 1, far, float(group * slab))
            gmean = over_group(mean) * (1.0 / per_group)
            d = mean - gmean
            gvar = over_group(m2 + total * d * d) * (1.0 / (per_group * total))
            return gmean, lax.rsqrt(gvar + EPS)

        own = kv[0, 0:slab].astype(F32)
        local_stats(own, 0)
        mean1, rstd1 = all_stats(0)

        for copy in small:
            copy.wait()

        scale1 = vec[0] * rstd1
        shift1 = vec[1]
        base1 = shift1 - mean1 * scale1
        key_scale = scale1 * (width**-0.5 * LOG2E)

        def make_queries(x, base):
            normed = ((x - mean1) * scale1 + shift1).astype(BF16)
            q = jnp.dot(normed, w4[0], preferred_element_type=F32).astype(BF16)
            t = lax.dot_general(q, w4[1], (((1,), (1,)), ((), ())), preferred_element_type=F32)
            q2[base : base + slab, :] = (t * key_scale).astype(BF16)

        state = {}

        def attend(who, first, count):
            base = who * slab
            keys = kv[first] if count == 1 else kv[first : first + count].reshape(count * 2 * slab, width)
            s = lax.dot_general(
                q2[base : base + slab, :], keys, (((1,), (1,)), ((), ())), preferred_element_type=F32
            )
            top = jnp.max(s, axis=-1, keepdims=True)
            if who in state:
                m, l = state[who]
                top = jnp.maximum(m, top)
                alpha = jnp.exp2(m - top)
            p = jnp.exp2(s - top).astype(BF16)
            psum = jnp.sum(p.astype(F32), axis=-1, keepdims=True)
            o = jnp.dot(p, keys, preferred_element_type=F32)
            if who in state:
                psum = l * alpha + psum
                o = acc[base : base + slab, :] * alpha + o
            acc[base : base + slab, :] = o
            state[who] = (top, psum)

        def finished(who):
            m, l = state[who]
            base = who * slab
            mean_key = acc[base : base + slab, :] / l
            return mean_key * scale1 + base1, m + jnp.log(l) * LOG2E

        diag = lax.broadcasted_iota(jnp.int32, (slab, width), 0) == lax.broadcasted_iota(
            jnp.int32, (slab, width), 1
        )

        OWN, OTHER = 0, 1
        forward_pair(rings, 0)
        make_queries(own, 0)
        to_partner.wait_recv()
        make_queries(xq[...].astype(F32), slab)
        forward_pair(rings, 1)
        sibs[1].start()
        sibs[2].start()
        sibs[0].wait_recv()
        attend(OTHER, 0, 1)
        attend(OWN, 0, 1)
        forward_pair(rings, 2)
        sibs[1].wait_recv()
        sibs[2].wait_recv()
        attend(OTHER, 1, 2)
        forward_pair(rings, 3)
        sibs[3].start()
        sibs[4].start()
        attend(OWN, 1, 2)
        sibs[3].wait_recv()
        sibs[4].wait_recv()
        forward_pair(rings, 4)
        attend(OTHER, 3, 2)
        attend(OWN, 3, 2)
        forward_pair(rings, 5)
        sibs[5].start()
        sibs[6].start()
        sibs[5].wait_recv()
        sibs[6].wait_recv()
        attend(OTHER, 5, 2)
        forward_pair(rings, 6)
        sibs[7].start()
        sibs[7].wait_recv()
        attend(OTHER, 7, 1)

        o, w = finished(OTHER)
        part[...] = o.astype(BF16)
        lse[...] = jnp.sum(jnp.where(diag, w, 0.0), axis=0, keepdims=True)
        part_copy = send(part, partin, misc_s.at[1], misc_r.at[1], partner)
        lse_copy = send(lse, lsein, misc_s.at[2], misc_r.at[2], partner)
        part_copy.start()
        lse_copy.start()
        attend(OWN, 5, 2)
        attend(OWN, 7, 1)
        o1, w1 = finished(OWN)
        lse_copy.wait_recv()
        w2 = jnp.sum(jnp.where(diag, lsein[...], 0.0), axis=1, keepdims=True)
        top = jnp.maximum(w1, w2)
        e1 = jnp.exp2(w1 - top)
        e2 = jnp.exp2(w2 - top)
        inv = 1.0 / (e1 + e2)
        o1 = o1 * (e1 * inv)
        part_copy.wait_recv()
        o = (o1 + partin[...].astype(F32) * (e2 * inv)).astype(BF16)
        attended = jnp.dot(o, w4[2], preferred_element_type=F32).astype(BF16)
        mixed = jnp.dot(attended, w4[3], preferred_element_type=F32) + vec[2] + kv[0, 0:slab].astype(F32)
        mixed = mixed.astype(BF16)
        curm[0:slab, :] = mixed
        top_row = pl.ds(0, cols)
        low_row = pl.ds(slab, cols)
        halos = [
            send(curm.at[pl.ds(0, slab)], earm.at[pl.ds(0, slab)], misc_s.at[3], misc_r.at[3], (later, h)),
            send(curm.at[top_row], curm.at[low_row], misc_s.at[4], misc_r.at[4], (f, above)),
            send(curm.at[top_row], earm.at[low_row], misc_s.at[5], misc_r.at[5], (later, above)),
        ]
        for copy in halos:
            copy.start()
        local_stats(mixed.astype(F32), 2)
        mean2, rstd2 = all_stats(2)
        scale2 = vec[3] * rstd2
        shift2 = vec[4]

        last_col = lax.broadcasted_iota(jnp.int32, (cols, width), 0) == cols - 1

        def activate(src, which, r, keep):
            x = src[r * cols : (r + 1) * cols, :].astype(F32)
            v = (x - mean2) * scale2 + shift2
            y = v / (1.0 + jnp.exp(-v))
            if keep is not None:
                y = jnp.where(keep, y, 0.0)
            act[which, 0, r * cols : (r + 1) * cols, :] = y.astype(BF16)
            y = jnp.where(last_col, 0.0, pltpu.roll(y, cols - 1, 0))
            act[which, 1, r * cols : (r + 1) * cols, :] = y.astype(BF16)

        has_below = h < nh - 1
        has_sooner = f > 0
        for r in range(rows):
            activate(curm, 0, r, None)
        for copy in halos:
            copy.wait_recv()
        activate(curm, 0, rows, has_below)
        for r in range(rows):
            activate(earm, 1, r, has_sooner)
        activate(earm, 1, rows, jnp.logical_and(has_below, has_sooner))
        up_copy.wait()

        taps = (((0, 1),), ((0, 2), (1, 0)))
        out_copies = []
        for b in range(2):
            for c in range(2):
                wins = [(rs, cs, q, r) for rs, q in taps[b] for cs, r in taps[c]]

                def windows(which):
                    parts = [act[which, cs, rs * cols : rs * cols + slab, :] for rs, cs, _, _ in wins]
                    return parts[0] if len(parts) == 1 else jnp.concatenate(parts, axis=1)

                def weights(p):
                    parts = [wupv[p, q, r] for _, _, q, r in wins]
                    return parts[0] if len(parts) == 1 else jnp.concatenate(parts, axis=0)

                current = windows(0)
                both = jnp.dot(
                    current,
                    jnp.concatenate([weights(0), weights(1)], axis=1),
                    preferred_element_type=F32,
                )
                y0 = both[:, 0:width] + jnp.dot(windows(1), weights(2), preferred_element_type=F32)
                for a, y in ((0, y0), (1, both[:, width:])):
                    y = y + vec[5]
                    for i in range(rows):
                        for n in range(lanes):
                            stage[a, i, n, pl.ds(c, cols, stride=2), :] = y[
                                i * cols : (i + 1) * cols, n * 128 : (n + 1) * 128
                            ]
            for a in range(2):
                for i in range(rows):
                    line = 2 * i + b
                    for n in range(lanes):
                        outv[a, line, :, n * 128 : (n + 1) * 128] = stage[a, i, n].astype(BF16)
                    copy = pltpu.make_async_copy(outv.at[a, line], out.at[a, line], outs.at[a, line])
                    copy.start()
                    out_copies.append(copy)

        for copy in out_copies:
            copy.wait()
        for copy in rings.values():
            copy.wait_send()
        for copy in sibs:
            copy.wait_send()
        to_partner.wait_send()
        part_copy.wait_send()
        lse_copy.wait_send()
        for copy in halos:
            copy.wait_send()

    def forward_pair(rings, step):
        for d in (True, False):
            rings[step, d].wait_recv()
            follow = step + 2
            if follow < 6:
                rings[follow, d].start()
            elif follow == 6 and d:
                rings[follow, d].start()
            elif follow == 7 and not d:
                rings[6, d].start()

    slab2 = 2 * slab
    dma = pltpu.SemaphoreType.DMA
    scratch = [
        pltpu.VMEM((NSLOT, slab2, width), BF16),
        pltpu.VMEM((slab, width), BF16),
        pltpu.VMEM((slab2, width), BF16),
        pltpu.VMEM((slab2, width), F32),
        pltpu.VMEM((slab, width), BF16),
        pltpu.VMEM((slab, width), BF16),
        pltpu.VMEM((1, width), F32),
        pltpu.VMEM((1, width), F32),
        pltpu.VMEM((4, width, width), BF16),
        pltpu.VMEM((3, 3, 3, width, width), BF16),
        pltpu.VMEM((6, 1, width), F32),
        pltpu.VMEM((4, group, 1, 2 * width), F32),
        pltpu.VMEM((slab + cols, width), BF16),
        pltpu.VMEM((slab + cols, width), BF16),
        pltpu.VMEM((2, 2, slab + cols, width), BF16),
        pltpu.VMEM((2, rows, lanes, 2 * cols, 128), F32),
        pltpu.VMEM((2, 2 * rows, 2 * cols, width), BF16),
        dma((4, group)),
        dma((4, group)),
        dma((7,)),
        dma((7,)),
        dma((7,)),
        dma((7,)),
        dma((NSLOT,)),
        dma((NSLOT,)),
        dma((6,)),
        dma((6,)),
        dma((11,)),
        dma,
        dma((2, 2 * rows)),
    ]
    return kernel, scratch


def solution(mesh):
    nf, nh = mesh.shape["frames"], mesh.shape["height"]

    def local(
        latent, first_gain, first_shift, query_weight, key_weight, value_weight, out_weight, out_bias,
        second_gain, second_shift, up_weight, up_bias,
    ):
        _, rows, cols, width = latent.shape
        kernel, scratch = make_kernel(nf, nh, rows, cols, width)

        def row(v):
            return v.reshape(1, width)

        out = pl.pallas_call(
            kernel,
            out_shape=jax.ShapeDtypeStruct((2, 2 * rows, 2 * cols, width), BF16),
            in_specs=[pl.BlockSpec(memory_space=pl.ANY)] * 12,
            out_specs=pl.BlockSpec(memory_space=pl.ANY),
            scratch_shapes=scratch,
            compiler_params=pltpu.CompilerParams(
                collective_id=0, has_side_effects=True, vmem_limit_bytes=56 * 1024 * 1024
            ),
            name="decoder_window",
        )(
            latent.reshape(rows * cols, width),
            row(first_gain), row(first_shift),
            query_weight, key_weight, value_weight, out_weight,
            row(out_bias), row(second_gain), row(second_shift),
            up_weight, row(up_bias),
        )
        return out

    whole = P("frames", "height", None, None)
    return jax.shard_map(
        local, mesh=mesh, in_specs=(whole,) + (P(),) * 11, out_specs=whole, check_vma=False
    )
```

time: 573 us -> 85.4 us (0.15)
  blocking collectives: 302 us -> 0 us
  waiting for transfers between devices: 187 us -> 0 us
  Pallas kernels: 0 us -> 74.5 us
  matrix products: 40.2 us -> 0 us
  other arithmetic: 18.8 us -> 0 us
  between operations: 13.9 us -> 0.01 us
  local copies, waits for them, and re-layouts: 3.35 us -> 10.5 us
  starting transfers between devices: 6.66 us -> 0 us
    psum x4 -> x0, blocking collectives: 302 us -> none  [the longest x2 156 us: group_norm(): mean = lax.psum(grouped(floats), ('frames', 'height')) / count]
    all_gather x2 -> x0, waiting for transfers between devices: 177 us -> none  [the longest x1 93.9 us: local(): lax.all_gather(keys, 'height', axis=1, tiled=True)]
    pallas_call x0 -> x1, Pallas kernels: none -> 74.5 us  [local(): pl.pallas_call(kernel, out_shape=jax.ShapeDtypeStruct((2, 2 * rows, 2 * c...]
    dot_general x32 -> x0, matrix products: 40.2 us -> none  [the longest x27 16 us: upsample_taps(): jnp.dot(window, weight[time_tap, row_tap, col_tap], preferred_element_typ...]
    ppermute x2 -> x0, waiting for transfers between devices: 9.61 us -> none  [passed_along(): lax.ppermute(value, axis, [(source, source + steps) for source in range(i...]
    reduce_sum x8 -> x0, other arithmetic: 9.51 us -> none  [the longest x1 6.87 us: local(): totals = jnp.sum(weights, axis=-1)]
    another operation x10 -> x0, other arithmetic: 7.32 us -> none  [the longest x4 2.86 us: upsample_taps(): row_list.append(jnp.stack(col_list, axis=2).reshape(rows, 2 * cols, width))]
    reshape x6, local copies, waits for them, and re-layouts: 0.63 us -> 7.52 us  [row(): return v.reshape(1, width)]
  transfers between devices with their start and end apart: 4 -> 0, of which waited for: 4 -> 0; matrix products, arithmetic and copies ran while one was open for 3% -> 0% of each run, Pallas kernels for 0% -> 0%
where the time goes in v1:
time: 85.4 us; the launch traced here: 85.1 us
  Pallas kernels  74.5 us (87%)
  local copies, waits for them, and re-layouts  10.5 us (12%)
    pallas_call x1, Pallas kernels, local(): pl.pallas_call(kernel, out_shape=jax.ShapeDtypeStruct((2, 2 * rows, 2 * c...  74.5 us
    reshape x6, local copies, waits for them, and re-layouts, row(): return v.reshape(1, width)  7.52 us
    unnamed x1, local copies, waits for them, and re-layouts  3.01 us

profile of v1, /device:TPU:1, one launch (start us, length us, event | category | flops | bytes accessed | tf_op | source)
XLA Modules:
  0.0 85.1 jit_solution(3087289349487353524)
XLA Ops:
  0.0 1.2 %reshape.22.g1 = f32[1,384]{1,0:T(1,128)} reshape(f32[384]{0:T(512)} %param.13) | data formatting | bytes 3072 | tf_op jit(solution)/shard_map/reshape | solution.py:416
  1.2 1.3 %reshape.23.s1 = f32[1,384]{1,0:T(1,128)} reshape(f32[384]{0:T(512)} %param.14) | data formatting | bytes 3072 | tf_op jit(solution)/shard_map/reshape | solution.py:416
  2.5 1.3 %reshape.24.ob = f32[1,384]{1,0:T(1,128)} reshape(f32[384]{0:T(512)} %param.19) | data formatting | bytes 3072 | tf_op jit(solution)/shard_map/reshape | solution.py:416
  3.8 1.2 %reshape.25.g2 = f32[1,384]{1,0:T(1,128)} reshape(f32[384]{0:T(512)} %param.20) | data formatting | bytes 3072 | tf_op jit(solution)/shard_map/reshape | solution.py:416
  5.0 1.3 %reshape.26.s2 = f32[1,384]{1,0:T(1,128)} reshape(f32[384]{0:T(512)} %param.21) | data formatting | bytes 3072 | tf_op jit(solution)/shard_map/reshape | solution.py:416
  6.3 1.3 %reshape.27.ub = f32[1,384]{1,0:T(1,128)} reshape(f32[384]{0:T(512)} %param.23) | data formatting | bytes 3072 | tf_op jit(solution)/shard_map/reshape | solution.py:416
  7.5 74.5 %decoder_window.1 = bf16[2,4,320,384]{3,2,1,0:T(8,128)(2,1)} custom-call(bf16[320,384]{1,0:T(8,128)(2,1)} %bitcast.1, f32[1,384]{1,0:T(1,128)} %reshape.22.g1, f32[1,384]{1,0:T(1,128)} %reshape.23.s1, bf16[384,384]{1,0:T(8,128)(2,1)} %wq.1, bf16[384,384]{1,0:T(8,128)(2,1)} %wk.1, bf16[384,384]{1,0:T(8,128)(2,1)} %wv.1, bf16[384,384]{1,0:T(8,128)(2,1)} %wo.1, ...), custom_call_target="tpu_custom_call" | custom-call | tf_op jit(solution)/shard_map/decoder_window/pallas_call | solution.py:418
  82.1 3.0 %copy.14 = bf16[2,4,320,384]{3,2,1,0:T(8,128)(2,1)} copy(bf16[2,4,320,384]{3,2,1,0:T(8,128)(2,1)} %decoder_window.1) | data formatting | bytes 3932160

commit v2 on v1

v2 whole, which is shorter than its diff:
```python
import jax
import jax.numpy as jnp
from jax import lax
from jax.experimental import pallas as pl
from jax.experimental.pallas import tpu as pltpu
from jax.sharding import PartitionSpec as P

GROUPS = 32
EPS = 1e-05
LOG2E = 1.4426950408889634
MESH = pl.DeviceIdType.MESH
BF16 = jnp.bfloat16
F32 = jnp.float32

NSLOT = 8
PIECES = 4


def make_kernel(nf, nh, rows, cols, width):
    slab = rows * cols
    piece = slab // PIECES
    steps = 3 * PIECES + PIECES // 2
    group = 16
    nx = nh // group
    total = float(nf * nh * slab)
    per_group = width // GROUPS
    lanes = width // 128

    def kernel(
        lat, g1, s1, wq, wk, wv, wo, ob, g2, s2, wup, ub, out,
        kv, xq, q2, acc, part, partin, lse, lsein, w4, wupv,
        g1v, s1v, obv, g2v, s2v, ubv, same,
        st, curm, earm, act, stage,
        st_s, st_r, kv_s, ring_r, sib_r, tail_s, misc_r, lse_s, loc, locv,
    ):
        vec = (g1v, s1v, obv, g2v, s2v, ubv)
        f = lax.axis_index("frames")
        h = lax.axis_index("height")
        xh = h // group
        k = h % group
        e = f * nx + xh

        def near(j):
            return (f, xh * group + (k + j) % group)

        def far(j):
            other = (e + j) % group
            return (other // nx, (other % nx) * group + k)

        right = near(2)
        left = near(group - 2)
        sibling = (f, xh * group + k + 1 - 2 * (k % 2))
        partner = (f, (h + group) % nh)
        above = (h + nh - 1) % nh
        below = (h + 1) % nh
        later = (f + 1) % nf
        sooner = (f + nf - 1) % nf

        def vrow(i):
            return vec[i][...].reshape(1, width)

        barrier = pltpu.get_barrier_semaphore()

        def greet(dev):
            pl.semaphore_signal(barrier, inc=1, device_id=dev, device_id_type=MESH)

        own_copy = pltpu.make_async_copy(lat, kv.at[0, pl.ds(0, slab)], loc.at[0])
        own_copy.start()

        def greet_both(j, carry):
            greet(near(j))
            greet(far(j))
            return carry

        lax.fori_loop(1, group, greet_both, 0)
        for dev in ((f, above), (f, below), (later, above), (sooner, below)):
            greet(dev)

        small = [
            pltpu.make_async_copy(src, w4.at[i], loc.at[1]) for i, src in enumerate((wq, wk, wv, wo))
        ]
        rows_in = [
            pltpu.make_async_copy(src, dst, locv.at[i])
            for i, (src, dst) in enumerate(zip((g1, s1, ob, g2, s2, ub), vec))
        ]
        for copy in small + rows_in:
            copy.start()
        up_copy = pltpu.make_async_copy(wup, wupv, loc.at[2])

        def send(src, dst, ss, rs, dev):
            return pltpu.make_async_remote_copy(
                src_ref=src, dst_ref=dst, send_sem=ss, recv_sem=rs, device_id=dev, device_id_type=MESH
            )

        def took(sem, size):
            pltpu.make_async_copy(size, size, sem).wait()

        def ring(step, to_right):
            hop = step // PIECES
            source = 0 if hop == 0 else (2 * hop - 1 if to_right else 2 * hop)
            target = 7 if hop == 3 else (2 * hop + 1 if to_right else 2 * hop + 2)
            at = pl.ds(((step % PIECES) + (0 if hop < 3 or to_right else PIECES // 2)) * piece, piece)
            return send(
                kv.at[source, at], kv.at[target, at], kv_s, ring_r.at[step], right if to_right else left
            )

        rings = {(s, d): ring(s, d) for s in range(steps) for d in (True, False)}

        def pass_on(first, last):
            for s in range(first, last):
                took(ring_r.at[s], kv.at[0, pl.ds(0, 2 * piece)])
                for d in (True, False):
                    onward = s + PIECES
                    if onward >= 3 * PIECES and not d:
                        onward -= PIECES // 2
                        if onward < 3 * PIECES:
                            continue
                    if onward < steps:
                        rings[onward, d].start()

        sibs = [
            send(kv.at[s, pl.ds(0, slab)], kv.at[s, pl.ds(slab, slab)], kv_s, sib_r.at[(s + 1) // 2], sibling)
            for s in range(NSLOT)
        ]
        to_partner = send(kv.at[0, pl.ds(0, slab)], xq, kv_s, misc_r.at[0], partner)

        def local_stats(x, slot):
            mean = jnp.sum(x, axis=0, keepdims=True) * (1.0 / slab)
            d = x - mean
            st[slot, 0] = jnp.concatenate([mean, jnp.sum(d * d, axis=0, keepdims=True)], axis=1)

        def messages(slot, peer):
            return [
                send(st.at[slot, 0], st.at[slot, j], st_s.at[slot], st_r.at[slot], peer(j))
                for j in range(1, group)
            ]

        def start(copies):
            for copy in copies:
                copy.start()

        def told(slot):
            took(st_r.at[slot], st.at[slot, pl.ds(1, group - 1)])

        def mates(i):
            took(sib_r.at[i], kv.at[0] if 0 < i < 4 else kv.at[0, pl.ds(0, slab)])

        def merged(slot, count):
            means = [st[slot, j, :, 0:width] for j in range(group)]
            mean = sum(means) * (1.0 / group)
            m2 = sum(st[slot, j, :, width : 2 * width] for j in range(group))
            return mean, m2 + count * sum((one - mean) * (one - mean) for one in means)

        def merge_to(slot, target, count):
            mean, m2 = merged(slot, count)
            st[target, 0] = jnp.concatenate([mean, m2], axis=1)

        line = lax.broadcasted_iota(jnp.int32, (16, width), 0)

        def over_group(row):
            high = row.astype(BF16).astype(F32)
            rest = row - high
            middle = rest.astype(BF16).astype(F32)
            pieces = jnp.where(line == 0, high, jnp.where(line == 1, middle, rest - middle))
            pieces = jnp.where(line < 3, pieces, 0.0).astype(BF16)
            sums = jnp.dot(pieces, same[...], preferred_element_type=F32)
            return jnp.sum(sums, axis=0, keepdims=True)

        def group_stats(slot):
            mean, m2 = merged(slot, float(group * slab))
            gmean = over_group(mean) * (1.0 / per_group)
            d = mean - gmean
            gvar = over_group(m2 + total * d * d) * (1.0 / (per_group * total))
            return gmean, lax.rsqrt(gvar + EPS)

        near1, far1 = messages(0, near), messages(1, far)
        far2, near2 = messages(2, far), messages(3, near)

        own_copy.wait()
        own = kv[0, 0:slab].astype(F32)
        local_stats(own, 0)
        grp_row = (lax.broadcasted_iota(jnp.int32, (width, width), 0) * 5462) >> 16
        grp_col = (lax.broadcasted_iota(jnp.int32, (width, width), 1) * 5462) >> 16
        same[...] = jnp.where(grp_row == grp_col, 1.0, 0.0).astype(BF16)
        pl.semaphore_wait(barrier, 2 * (group - 1) + 4)
        start(near1)
        for s in range(PIECES):
            rings[s, True].start()
            rings[s, False].start()
        to_partner.start()
        sibs[0].start()
        up_copy.start()
        took(loc.at[1], w4)
        for copy in rows_in:
            copy.wait()
        value_out = jnp.dot(w4[2], w4[3], preferred_element_type=F32).astype(BF16)
        w4[2] = value_out
        told(0)
        merge_to(0, 1, float(slab))
        start(far1)
        pass_on(0, 4)
        start(sibs[1:3])
        pass_on(4, 5)
        told(1)
        mean1, rstd1 = group_stats(1)
        pass_on(5, 6)
        scale1 = vrow(0) * rstd1
        shift1 = vrow(1)
        base1 = shift1 - mean1 * scale1
        key_scale = scale1 * (width**-0.5 * LOG2E)

        def make_queries(x, base):
            normed = ((x - mean1) * scale1 + shift1).astype(BF16)
            q = jnp.dot(normed, w4[0], preferred_element_type=F32).astype(BF16)
            t = lax.dot_general(q, w4[1], (((1,), (1,)), ((), ())), preferred_element_type=F32)
            q2[base : base + slab, :] = (t * key_scale).astype(BF16)

        state = {}

        def attend_rows(base, n, m, l, first, count):
            at = slice(base, base + n)
            keys = kv[first : first + count].reshape(count * 2 * slab, width)
            s = lax.dot_general(
                q2[at, :], keys, (((1,), (1,)), ((), ())), preferred_element_type=F32
            )
            top = jnp.max(s, axis=-1, keepdims=True)
            if m is not None:
                top = jnp.maximum(m, top)
                alpha = jnp.exp2(m - top)
            p = jnp.exp2(s - top).astype(BF16)
            psum = jnp.sum(p.astype(F32), axis=-1, keepdims=True)
            o = jnp.dot(p, keys, preferred_element_type=F32)
            if m is not None:
                psum = l * alpha + psum
                o = acc[at, :] * alpha + o
            acc[at, :] = o
            return top, psum

        def attend(who, first, count):
            m, l = state.get(who, (None, None))
            state[who] = attend_rows(who * slab, slab, m, l, first, count)

        def finished(base, n, m, l):
            mean_key = acc[base : base + n, :] / l
            return (mean_key * scale1 + base1).astype(BF16), m + jnp.log(l) * LOG2E

        diag = lax.broadcasted_iota(jnp.int32, (slab, width), 0) == lax.broadcasted_iota(
            jnp.int32, (slab, width), 1
        )

        OWN, OTHER = 0, 1
        make_queries(own, 0)
        pass_on(6, 7)
        to_partner.wait_recv()
        make_queries(xq[...].astype(F32), slab)
        pass_on(7, 8)
        start(sibs[3:5])
        mates(0)
        attend(OTHER, 0, 1)
        mates(1)
        attend(OTHER, 1, 2)
        pass_on(8, 9)
        mates(2)
        attend(OTHER, 3, 2)
        pass_on(9, 10)
        attend(OWN, 0, 1)
        pass_on(10, 11)
        attend(OWN, 1, 2)
        pass_on(11, 12)
        start(sibs[5:7])
        attend(OWN, 3, 2)
        pass_on(12, 13)
        mates(3)
        attend(OTHER, 5, 2)
        pass_on(13, 14)
        sibs[7].start()
        mates(4)
        halfway = slab // 2
        halves = [slice(0, halfway), slice(halfway, slab)]
        part_copies = [
            send(part.at[pl.ds(i * halfway, halfway)], partin.at[pl.ds(i * halfway, halfway)], tail_s, misc_r.at[1 + i], partner)
            for i in range(2)
        ]
        lse_copy = send(lse, lsein, lse_s, misc_r.at[3], partner)
        m, l = state[OTHER]
        weights = []
        for i, at in enumerate(halves):
            top, total_l = attend_rows(slab + i * halfway, halfway, m[at], l[at], 7, 1)
            part[at, :], w = finished(slab + i * halfway, halfway, top, total_l)
            weights.append(w)
            if i == 1:
                w = jnp.concatenate(weights, axis=0)
                lse[...] = jnp.sum(jnp.where(diag, w, 0.0), axis=0, keepdims=True)
                lse_copy.start()
            part_copies[i].start()
        attend(OWN, 5, 2)
        attend(OWN, 7, 1)
        o1, w1 = finished(0, slab, *state[OWN])
        y1 = jnp.dot(o1, w4[2], preferred_element_type=F32)
        base = kv[0, 0:slab].astype(F32) + vrow(2)
        lse_copy.wait_recv()
        w2 = jnp.sum(jnp.where(diag, lsein[...], 0.0), axis=1, keepdims=True)
        top = jnp.maximum(w1, w2)
        e1 = jnp.exp2(w1 - top)
        e2 = jnp.exp2(w2 - top)
        inv = 1.0 / (e1 + e2)
        base = base + y1 * (e1 * inv)
        e2 = e2 * inv
        mixed = []
        for i, at in enumerate(halves):
            part_copies[i].wait_recv()
            y2 = jnp.dot(partin[at, :], w4[2], preferred_element_type=F32)
            mixed.append((base[at] + y2 * e2[at]).astype(BF16))
        mixed = jnp.concatenate(mixed, axis=0)
        curm[0:slab, :] = mixed
        top_row = pl.ds(0, cols)
        low_row = pl.ds(slab, cols)
        halos = [
            send(curm.at[pl.ds(0, slab)], earm.at[pl.ds(0, slab)], tail_s, misc_r.at[4], (later, h)),
            send(curm.at[top_row], curm.at[low_row], tail_s, misc_r.at[4], (f, above)),
            send(curm.at[top_row], earm.at[low_row], tail_s, misc_r.at[4], (later, above)),
        ]
        local_stats(mixed.astype(F32), 2)
        start(far2)
        start(halos)
        told(2)
        merge_to(2, 3, float(slab))
        start(near2)
        told(3)
        mean2, rstd2 = group_stats(3)
        scale2 = vrow(3) * rstd2
        shift2 = vrow(4)

        last_col = lax.broadcasted_iota(jnp.int32, (cols, width), 0) == cols - 1

        def activate(src, which, r, keep):
            x = src[r * cols : (r + 1) * cols, :].astype(F32)
            v = (x - mean2) * scale2 + shift2
            y = v / (1.0 + jnp.exp(-v))
            if keep is not None:
                y = jnp.where(keep, y, 0.0)
            act[which, 0, r * cols : (r + 1) * cols, :] = y.astype(BF16)
            y = jnp.where(last_col, 0.0, pltpu.roll(y, cols - 1, 0))
            act[which, 1, r * cols : (r + 1) * cols, :] = y.astype(BF16)

        has_below = h < nh - 1
        has_sooner = f > 0
        for r in range(rows):
            activate(curm, 0, r, None)
        took(misc_r.at[4], kv.at[0])
        activate(curm, 0, rows, has_below)
        for r in range(rows):
            activate(earm, 1, r, has_sooner)
        activate(earm, 1, rows, jnp.logical_and(has_below, has_sooner))
        up_copy.wait()

        taps = (((0, 1),), ((0, 2), (1, 0)))
        for b in range(2):
            for c in range(2):
                wins = [(rs, cs, q, r) for rs, q in taps[b] for cs, r in taps[c]]

                def windows(which):
                    parts = [act[which, cs, rs * cols : rs * cols + slab, :] for rs, cs, _, _ in wins]
                    return parts[0] if len(parts) == 1 else jnp.concatenate(parts, axis=1)

                def weights(p):
                    parts = [wupv[p, q, r] for _, _, q, r in wins]
                    return parts[0] if len(parts) == 1 else jnp.concatenate(parts, axis=0)

                current = windows(0)
                both = jnp.dot(
                    current,
                    jnp.concatenate([weights(0), weights(1)], axis=1),
                    preferred_element_type=F32,
                )
                y0 = both[:, 0:width] + jnp.dot(windows(1), weights(2), preferred_element_type=F32)
                for a, y in ((0, y0), (1, both[:, width:])):
                    y = y + vrow(5)
                    for i in range(rows):
                        for n in range(lanes):
                            stage[a, i, n, pl.ds(c, cols, stride=2), :] = y[
                                i * cols : (i + 1) * cols, n * 128 : (n + 1) * 128
                            ]
            for a in range(2):
                for i in range(rows):
                    for n in range(lanes):
                        out[a, 2 * i + b, :, n * 128 : (n + 1) * 128] = stage[a, i, n].astype(BF16)

        took(kv_s, kv)
        took(tail_s, act.at[0])
        lse_copy.wait_send()
        for slot in range(4):
            took(st_s.at[slot], st.at[slot, pl.ds(1, group - 1)])

    slab2 = 2 * slab
    dma = pltpu.SemaphoreType.DMA
    scratch = [
        pltpu.VMEM((NSLOT, slab2, width), BF16),
        pltpu.VMEM((slab, width), BF16),
        pltpu.VMEM((slab2, width), BF16),
        pltpu.VMEM((slab2, width), F32),
        pltpu.VMEM((slab, width), BF16),
        pltpu.VMEM((slab, width), BF16),
        pltpu.VMEM((1, width), F32),
        pltpu.VMEM((1, width), F32),
        pltpu.VMEM((4, width, width), BF16),
        pltpu.VMEM((3, 3, 3, width, width), BF16),
        *[pltpu.VMEM((width,), F32)] * 6,
        pltpu.VMEM((width, width), BF16),
        pltpu.VMEM((4, group, 1, 2 * width), F32),
        pltpu.VMEM((slab + cols, width), BF16),
        pltpu.VMEM((slab + cols, width), BF16),
        pltpu.VMEM((2, 2, slab + cols, width), BF16),
        pltpu.VMEM((2, rows, lanes, 2 * cols, 128), F32),
        dma((4,)),
        dma((4,)),
        dma,
        dma((steps,)),
        dma((5,)),
        dma,
        dma((5,)),
        dma,
        dma((3,)),
        dma((6,)),
    ]
    return kernel, scratch


def solution(mesh):
    nf, nh = mesh.shape["frames"], mesh.shape["height"]

    def local(
        latent, first_gain, first_shift, query_weight, key_weight, value_weight, out_weight, out_bias,
        second_gain, second_shift, up_weight, up_bias,
    ):
        _, rows, cols, width = latent.shape
        kernel, scratch = make_kernel(nf, nh, rows, cols, width)

        out = pl.pallas_call(
            kernel,
            out_shape=pltpu.VMEM((2, 2 * rows, 2 * cols, width), BF16),
            in_specs=[pl.BlockSpec(memory_space=pl.ANY)] * 12,
            out_specs=pl.BlockSpec(memory_space=pltpu.VMEM),
            scratch_shapes=scratch,
            compiler_params=pltpu.CompilerParams(
                collective_id=0, has_side_effects=True, vmem_limit_bytes=56 * 1024 * 1024
            ),
            name="decoder_window",
        )(
            latent.reshape(rows * cols, width),
            first_gain, first_shift,
            query_weight, key_weight, value_weight, out_weight,
            out_bias, second_gain, second_shift,
            up_weight, up_bias,
        )
        return out

    whole = P("frames", "height", None, None)
    return jax.shard_map(
        local, mesh=mesh, in_specs=(whole,) + (P(),) * 11, out_specs=whole, check_vma=False
    )
```

time: 85.4 us -> 64.9 us (0.76)
  the two profiles are of different devices: /device:TPU:1 before, /device:TPU:5 now
where the time goes in v2:
time: 64.9 us; the launch traced here: 64.8 us
  Pallas kernels  63.5 us (98%)
  local copies, waits for them, and re-layouts  1.27 us (2%)
    pallas_call x1, Pallas kernels, local(): pl.pallas_call(kernel, out_shape=pltpu.VMEM((2, 2 * rows, 2 * cols, width...  63.5 us

profile of v2, /device:TPU:5, one launch (start us, length us, event | category | flops | bytes accessed | tf_op | source)
XLA Modules:
  0.0 64.8 jit_solution(7385244548931211950)
XLA Ops:
  0.0 63.5 %decoder_window.1 = bf16[2,4,320,384]{3,2,1,0:T(8,128)(2,1)S(1)} custom-call(bf16[320,384]{1,0:T(8,128)(2,1)} %bitcast.1, f32[384]{0:T(512)} %g1.1, f32[384]{0:T(512)} %s1_.1, bf16[384,384]{1,0:T(8,128)(2,1)} %wq.1, bf16[384,384]{1,0:T(8,128)(2,1)} %wk.1, bf16[384,384]{1,0:T(8,128)(2,1)} %wv.1, bf16[384,384]{1,0:T(8,128)(2,1)} %wo.1, f32[384]{0:T(512)} %ob.1, ...), custom_call_target="tpu_custom_call" | custom-call | tf_op jit(solution)/shard_map/decoder_window/pallas_call | solution.py:439
  63.5 1.3 %copy.14 = bf16[2,4,320,384]{3,2,1,0:T(8,128)(2,1)} copy(bf16[2,4,320,384]{3,2,1,0:T(8,128)(2,1)S(1)} %decoder_window.1) | data formatting | bytes 3932160

commit v3 on v2

--- a/solution.py
+++ b/solution.py
@@ -54,7 +54,6 @@
         above = (h + nh - 1) % nh
         below = (h + 1) % nh
         later = (f + 1) % nf
-        sooner = (f + nf - 1) % nf
 
         def vrow(i):
             return vec[i][...].reshape(1, width)
@@ -73,7 +72,7 @@
             return carry
 
         lax.fori_loop(1, group, greet_both, 0)
-        for dev in ((f, above), (f, below), (later, above), (sooner, below)):
+        for dev in ((f, above), (f, below)):
             greet(dev)
 
         small = [
@@ -107,7 +106,7 @@
         rings = {(s, d): ring(s, d) for s in range(steps) for d in (True, False)}
 
         def pass_on(first, last):
-            for s in range(first, last):
+            for s in range(first * PIECES // 4, last * PIECES // 4):
                 took(ring_r.at[s], kv.at[0, pl.ds(0, 2 * piece)])
                 for d in (True, False):
                     onward = s + PIECES
@@ -132,7 +131,7 @@
         def messages(slot, peer):
             return [
                 send(st.at[slot, 0], st.at[slot, j], st_s.at[slot], st_r.at[slot], peer(j))
-                for j in range(1, group)
+                for j in sorted(range(1, group), key=lambda j: abs(j - group // 2))
             ]
 
         def start(copies):
@@ -182,7 +181,7 @@
         grp_row = (lax.broadcasted_iota(jnp.int32, (width, width), 0) * 5462) >> 16
         grp_col = (lax.broadcasted_iota(jnp.int32, (width, width), 1) * 5462) >> 16
         same[...] = jnp.where(grp_row == grp_col, 1.0, 0.0).astype(BF16)
-        pl.semaphore_wait(barrier, 2 * (group - 1) + 4)
+        pl.semaphore_wait(barrier, 2 * (group - 1) + 2)
         start(near1)
         for s in range(PIECES):
             rings[s, True].start()
@@ -315,17 +314,21 @@
         curm[0:slab, :] = mixed
         top_row = pl.ds(0, cols)
         low_row = pl.ds(slab, cols)
+        bottom_row = pl.ds(cols, slab - cols)
         halos = [
-            send(curm.at[pl.ds(0, slab)], earm.at[pl.ds(0, slab)], tail_s, misc_r.at[4], (later, h)),
-            send(curm.at[top_row], curm.at[low_row], tail_s, misc_r.at[4], (f, above)),
-            send(curm.at[top_row], earm.at[low_row], tail_s, misc_r.at[4], (later, above)),
+            send(curm.at[top_row], earm.at[top_row], tail_s, misc_r.at[4], (later, h)),
+            send(curm.at[bottom_row], earm.at[bottom_row], tail_s, misc_r.at[5], (later, h)),
+            send(curm.at[top_row], curm.at[low_row], tail_s, misc_r.at[6], (f, above)),
+            send(earm.at[top_row], earm.at[low_row], tail_s, misc_r.at[7], (f, above)),
         ]
         local_stats(mixed.astype(F32), 2)
         start(far2)
-        start(halos)
+        start(halos[:3])
         told(2)
         merge_to(2, 3, float(slab))
         start(near2)
+        halos[0].wait_recv()
+        halos[3].start()
         told(3)
         mean2, rstd2 = group_stats(3)
         scale2 = vrow(3) * rstd2
@@ -347,7 +350,8 @@
         has_sooner = f > 0
         for r in range(rows):
             activate(curm, 0, r, None)
-        took(misc_r.at[4], kv.at[0])
+        for copy in halos[1:]:
+            copy.wait_recv()
         activate(curm, 0, rows, has_below)
         for r in range(rows):
             activate(earm, 1, r, has_sooner)
@@ -418,7 +422,7 @@
         dma((steps,)),
         dma((5,)),
         dma,
-        dma((5,)),
+        dma((8,)),
         dma,
         dma((3,)),
         dma((6,)),

time: 64.9 us -> 61.3 us (0.945)
  the two profiles are of different devices: /device:TPU:5 before, /device:TPU:1 now
where the time goes in v3:
time: 61.3 us; the launch traced here: 61.2 us
  Pallas kernels  59.9 us (98%)
  local copies, waits for them, and re-layouts  1.27 us (2%)
    pallas_call x1, Pallas kernels, local(): pl.pallas_call(kernel, out_shape=pltpu.VMEM((2, 2 * rows, 2 * cols, width...  59.9 us
    unnamed x1, local copies, waits for them, and re-layouts  1.27 us

profile of v3, /device:TPU:1, one launch (start us, length us, event | category | flops | bytes accessed | tf_op | source)
XLA Modules:
  0.0 61.2 jit_solution(10476072060225210532)
XLA Ops:
  0.0 59.9 %decoder_window.1 = bf16[2,4,320,384]{3,2,1,0:T(8,128)(2,1)S(1)} custom-call(bf16[320,384]{1,0:T(8,128)(2,1)} %bitcast.1, f32[384]{0:T(512)} %g1.1, f32[384]{0:T(512)} %s1_.1, bf16[384,384]{1,0:T(8,128)(2,1)} %wq.1, bf16[384,384]{1,0:T(8,128)(2,1)} %wk.1, bf16[384,384]{1,0:T(8,128)(2,1)} %wv.1, bf16[384,384]{1,0:T(8,128)(2,1)} %wo.1, f32[384]{0:T(512)} %ob.1, ...), custom_call_target="tpu_custom_call" | custom-call | tf_op jit(solution)/shard_map/decoder_window/pallas_call | solution.py:443
  59.9 1.3 %copy.14 = bf16[2,4,320,384]{3,2,1,0:T(8,128)(2,1)} copy(bf16[2,4,320,384]{3,2,1,0:T(8,128)(2,1)S(1)} %decoder_window.1) | data formatting | bytes 3932160

commit v4 on v3

--- a/solution.py
+++ b/solution.py
@@ -29,7 +29,7 @@
     def kernel(
         lat, g1, s1, wq, wk, wv, wo, ob, g2, s2, wup, ub, out,
         kv, xq, q2, acc, part, partin, lse, lsein, w4, wupv,
-        g1v, s1v, obv, g2v, s2v, ubv, same,
+        g1v, s1v, obv, g2v, s2v, ubv, same, member,
         st, curm, earm, act, stage,
         st_s, st_r, kv_s, ring_r, sib_r, tail_s, misc_r, lse_s, loc, locv,
     ):
@@ -123,10 +123,29 @@
         ]
         to_partner = send(kv.at[0, pl.ds(0, slab)], xq, kv_s, misc_r.at[0], partner)
 
+        line = lax.broadcasted_iota(jnp.int32, (16, width), 0)
+
+        def pieces_of(row, first):
+            high = row.astype(BF16).astype(F32)
+            rest = row - high
+            middle = rest.astype(BF16).astype(F32)
+            at = line[:, 0 : row.shape[1]] - first
+            rows_ = jnp.where(at == 0, high, jnp.where(at == 1, middle, rest - middle))
+            return jnp.where((at >= 0) & (at < 3), rows_, 0.0)
+
+        def sums(pieces, matrix):
+            return jnp.dot(pieces.astype(BF16), matrix, preferred_element_type=F32)
+
         def local_stats(x, slot):
             mean = jnp.sum(x, axis=0, keepdims=True) * (1.0 / slab)
+            pieces = pieces_of(mean, 0)
+            spread = jnp.sum(sums(pieces, same[...]), axis=0, keepdims=True) * (1.0 / per_group)
+            gmean = jnp.sum(sums(pieces, member[...]), axis=0, keepdims=True) * (1.0 / per_group)
             d = x - mean
-            st[slot, 0] = jnp.concatenate([mean, jnp.sum(d * d, axis=0, keepdims=True)], axis=1)
+            apart = mean - spread
+            m2 = jnp.sum(d * d, axis=0, keepdims=True) + float(slab) * apart * apart
+            m2 = jnp.sum(sums(pieces_of(m2, 0), member[...]), axis=0, keepdims=True)
+            st[slot, 0] = jnp.concatenate([gmean, m2], axis=1)
 
         def messages(slot, peer):
             return [
@@ -144,43 +163,40 @@
         def mates(i):
             took(sib_r.at[i], kv.at[0] if 0 < i < 4 else kv.at[0, pl.ds(0, slab)])
 
-        def merged(slot, count):
-            means = [st[slot, j, :, 0:width] for j in range(group)]
+        def merged(slot, devices):
+            means = [st[slot, j, :, 0:128] for j in range(group)]
             mean = sum(means) * (1.0 / group)
-            m2 = sum(st[slot, j, :, width : 2 * width] for j in range(group))
+            m2 = sum(st[slot, j, :, 128:256] for j in range(group))
+            count = float(devices * slab * per_group)
             return mean, m2 + count * sum((one - mean) * (one - mean) for one in means)
 
-        def merge_to(slot, target, count):
-            mean, m2 = merged(slot, count)
+        def merge_to(slot, target):
+            mean, m2 = merged(slot, 1)
             st[target, 0] = jnp.concatenate([mean, m2], axis=1)
 
-        line = lax.broadcasted_iota(jnp.int32, (16, width), 0)
-
-        def over_group(row):
-            high = row.astype(BF16).astype(F32)
-            rest = row - high
-            middle = rest.astype(BF16).astype(F32)
-            pieces = jnp.where(line == 0, high, jnp.where(line == 1, middle, rest - middle))
-            pieces = jnp.where(line < 3, pieces, 0.0).astype(BF16)
-            sums = jnp.dot(pieces, same[...], preferred_element_type=F32)
-            return jnp.sum(sums, axis=0, keepdims=True)
-
         def group_stats(slot):
-            mean, m2 = merged(slot, float(group * slab))
-            gmean = over_group(mean) * (1.0 / per_group)
-            d = mean - gmean
-            gvar = over_group(m2 + total * d * d) * (1.0 / (per_group * total))
-            return gmean, lax.rsqrt(gvar + EPS)
+            gmean, m2 = merged(slot, group)
+            grstd = lax.rsqrt(m2 * (1.0 / (per_group * total)) + EPS)
+            pieces = pieces_of(gmean, 0) + pieces_of(grstd, 8)
+            wide = lax.dot_general(
+                pieces.astype(BF16), member[...], (((1,), (1,)), ((), ())), preferred_element_type=F32
+            )
+            return (
+                jnp.sum(wide[0:8], axis=0, keepdims=True),
+                jnp.sum(wide[8:16], axis=0, keepdims=True),
+            )
 
         near1, far1 = messages(0, near), messages(1, far)
         far2, near2 = messages(2, far), messages(3, near)
 
         own_copy.wait()
         own = kv[0, 0:slab].astype(F32)
-        local_stats(own, 0)
         grp_row = (lax.broadcasted_iota(jnp.int32, (width, width), 0) * 5462) >> 16
         grp_col = (lax.broadcasted_iota(jnp.int32, (width, width), 1) * 5462) >> 16
         same[...] = jnp.where(grp_row == grp_col, 1.0, 0.0).astype(BF16)
+        grp_lane = lax.broadcasted_iota(jnp.int32, (width, 128), 1)
+        member[...] = jnp.where(grp_row[:, 0:128] == grp_lane, 1.0, 0.0).astype(BF16)
+        local_stats(own, 0)
         pl.semaphore_wait(barrier, 2 * (group - 1) + 2)
         start(near1)
         for s in range(PIECES):
@@ -195,7 +211,7 @@
         value_out = jnp.dot(w4[2], w4[3], preferred_element_type=F32).astype(BF16)
         w4[2] = value_out
         told(0)
-        merge_to(0, 1, float(slab))
+        merge_to(0, 1)
         start(far1)
         pass_on(0, 4)
         start(sibs[1:3])
@@ -325,7 +341,7 @@
         start(far2)
         start(halos[:3])
         told(2)
-        merge_to(2, 3, float(slab))
+        merge_to(2, 3)
         start(near2)
         halos[0].wait_recv()
         halos[3].start()
@@ -411,7 +427,8 @@
         pltpu.VMEM((3, 3, 3, width, width), BF16),
         *[pltpu.VMEM((width,), F32)] * 6,
         pltpu.VMEM((width, width), BF16),
-        pltpu.VMEM((4, group, 1, 2 * width), F32),
+        pltpu.VMEM((width, 128), BF16),
+        pltpu.VMEM((4, group, 1, 256), F32),
         pltpu.VMEM((slab + cols, width), BF16),
         pltpu.VMEM((slab + cols, width), BF16),
         pltpu.VMEM((2, 2, slab + cols, width), BF16),

time: 61.3 us -> 60.3 us (0.984)
  Pallas kernels: 59.9 us -> 59 us
    pallas_call x1, Pallas kernels: 59.9 us -> 59 us  [local(): pl.pallas_call(kernel, out_shape=pltpu.VMEM((2, 2 * rows, 2 * cols, width...]
where the time goes in v4:
time: 60.3 us; the launch traced here: 60.2 us
  Pallas kernels  59 us (98%)
  local copies, waits for them, and re-layouts  1.27 us (2%)
    pallas_call x1, Pallas kernels, local(): pl.pallas_call(kernel, out_shape=pltpu.VMEM((2, 2 * rows, 2 * cols, width...  59 us
    unnamed x1, local copies, waits for them, and re-layouts  1.27 us

profile of v4, /device:TPU:1, one launch (start us, length us, event | category | flops | bytes accessed | tf_op | source)
XLA Modules:
  0.0 60.2 jit_solution(4937568081536065096)
XLA Ops:
  0.0 59.0 %decoder_window.1 = bf16[2,4,320,384]{3,2,1,0:T(8,128)(2,1)S(1)} custom-call(bf16[320,384]{1,0:T(8,128)(2,1)} %bitcast.1, f32[384]{0:T(512)} %g1.1, f32[384]{0:T(512)} %s1_.1, bf16[384,384]{1,0:T(8,128)(2,1)} %wq.1, bf16[384,384]{1,0:T(8,128)(2,1)} %wk.1, bf16[384,384]{1,0:T(8,128)(2,1)} %wv.1, bf16[384,384]{1,0:T(8,128)(2,1)} %wo.1, f32[384]{0:T(512)} %ob.1, ...), custom_call_target="tpu_custom_call" | custom-call | tf_op jit(solution)/shard_map/decoder_window/pallas_call | solution.py:460
  59.0 1.3 %copy.14 = bf16[2,4,320,384]{3,2,1,0:T(8,128)(2,1)} copy(bf16[2,4,320,384]{3,2,1,0:T(8,128)(2,1)S(1)} %decoder_window.1) | data formatting | bytes 3932160

commit v5 on v4

--- a/solution.py
+++ b/solution.py
@@ -339,10 +339,11 @@
         ]
         local_stats(mixed.astype(F32), 2)
         start(far2)
-        start(halos[:3])
+        start(halos[:2])
         told(2)
         merge_to(2, 3)
         start(near2)
+        halos[2].start()
         halos[0].wait_recv()
         halos[3].start()
         told(3)

time: 60.3 us -> 60.3 us (level)
  no operation moved by 1% of the time
where the time goes in v5:
time: 60.3 us; the launch traced here: 60.2 us
  Pallas kernels  59 us (98%)
  local copies, waits for them, and re-layouts  1.27 us (2%)
    pallas_call x1, Pallas kernels, local(): pl.pallas_call(kernel, out_shape=pltpu.VMEM((2, 2 * rows, 2 * cols, width...  59 us
    unnamed x1, local copies, waits for them, and re-layouts  1.27 us

profile of v5, /device:TPU:1, one launch (start us, length us, event | category | flops | bytes accessed | tf_op | source)
XLA Modules:
  0.0 60.2 jit_solution(4933450047364519249)
XLA Ops:
  0.0 59.0 %decoder_window.1 = bf16[2,4,320,384]{3,2,1,0:T(8,128)(2,1)S(1)} custom-call(bf16[320,384]{1,0:T(8,128)(2,1)} %bitcast.1, f32[384]{0:T(512)} %g1.1, f32[384]{0:T(512)} %s1_.1, bf16[384,384]{1,0:T(8,128)(2,1)} %wq.1, bf16[384,384]{1,0:T(8,128)(2,1)} %wk.1, bf16[384,384]{1,0:T(8,128)(2,1)} %wv.1, bf16[384,384]{1,0:T(8,128)(2,1)} %wo.1, f32[384]{0:T(512)} %ob.1, ...), custom_call_target="tpu_custom_call" | custom-call | tf_op jit(solution)/shard_map/decoder_window/pallas_call | solution.py:461
  59.0 1.3 %copy.14 = bf16[2,4,320,384]{3,2,1,0:T(8,128)(2,1)} copy(bf16[2,4,320,384]{3,2,1,0:T(8,128)(2,1)S(1)} %decoder_window.1) | data formatting | bytes 3932160
